TPU v7x, 32 devices: a whole 2x2x4 slice. The times are simulated.
32 devices in a mesh: scen: 16 (over z, y, x), net: 2 (over core).
Axes of the slice: x: 2, y: 2, z: 4, core: 2. Of those that a mesh axis runs over, the one named last changes fastest.
Arguments:
- prior_mean: float32 [64, 32, 128], P('scen', 'net'), may hold values from 0 to 2
- multipliers: float32 [64, 32, 128], P('scen', 'net'), may hold values from -4 to 4
- demand: float32 [64, 32, 128], P('scen', 'net'), may hold values from -6 to 6
- linear_cost: float32 [32, 128], P('net'), may hold values from -4 to 4
- penalty: float32 [32, 128], P('net'), may hold values from 0.5 to 4
- constraint_blocks: float32 [32, 4, 128, 128], P('net'), may hold values from -0.25 to 0.25
- block_columns: int32 [32, 4], P('net'), may hold values from 0 to 19, as said below
- block_section: int32 [32], P('net'), may hold values from 0 to 5
Outputs:
- consensus: float32 [64, 32, 128], P('scen', 'net')
- new_multipliers: float32 [64, 32, 128], P('scen', 'net')
Inputs may be any that keep to these rules, and one draw needn't show every extreme that they name: block_columns[i, 0] is 2 plus the position of block i among its partition's 16 blocks; every other entry differs from it by 1 to 2 blocks; in each partition the first block reaches 2 blocks before it and the last one 2 blocks after it.
All inputs are finite; a program needn't handle non-finite values.
Results may differ from a plain program's by a relative error of at most 0.00015.
Values sent between devices are 32-bit elements; how exact they have to be, the bound alone decides.
A program may use at most 64 MiB of HBM per device.

v0:
```python
import jax
import jax.numpy as jnp
from jax import lax
from jax.sharding import PartitionSpec as P

HB = 2
ITERS = 2


exact_mode = lax.Precision.HIGHEST


def extended_2(block, sides, width):
    for axis, dim in sides:
        count = lax.axis_size(axis)
        forward = [(i, i + 1) for i in range(count - 1)]
        backward = [(target, source) for source, target in forward]
        low = lax.ppermute(
            lax.slice_in_dim(block, block.shape[dim] - width, None, axis=dim), axis, forward
        )
        high = lax.ppermute(lax.slice_in_dim(block, 0, width, axis=dim), axis, backward)
        block = jnp.concatenate([low, block, high], axis=dim)
    return block


def shifted(block, axis, distance):
    devices = range(lax.axis_size(axis))
    route = [(i - distance, i) for i in devices if i - distance in devices]
    return lax.ppermute(block, axis, route)


def from_partner(value, axis, bit):
    mask = 2**bit
    pairs = [(source, source ^ mask) for source in range(lax.axis_size(axis))]
    return lax.ppermute(value, axis, pairs)


def inner_sum(left_side, right_side):
    return jnp.sum(left_side * right_side, axis=(1, 2))


def body(
    prior_mean,
    multipliers,
    demand,
    linear_cost,
    penalty,
    constraint_blocks,
    block_columns,
    block_section,
):
    scen_count = prior_mean.shape[0]
    block_count = prior_mean.shape[1]
    one_hot = (
        block_columns[:, :, None]
        == jnp.arange(block_count + 2 * HB, dtype=jnp.int32)[None, None, :]
    ).astype(jnp.float32)

    def forward(values):
        extended = extended_2(values, (("net", 1),), HB)
        picked = jnp.einsum("ike,sec->sikc", one_hot, extended, precision=exact_mode)
        return jnp.einsum("ikrc,sikc->sir", constraint_blocks, picked, precision=exact_mode)

    def apply_transpose(values):
        block_terms = jnp.einsum("ikrc,sir->sikc", constraint_blocks, values, precision=exact_mode)
        spread = jnp.einsum("ike,sikc->sec", one_hot, block_terms, precision=exact_mode)
        interior = spread[:, HB : HB + block_count]
        from_above = shifted(spread[:, :HB], "net", -1)
        from_below = shifted(spread[:, HB + block_count :], "net", 1)
        interior = interior.at[:, block_count - HB :].add(from_above)
        return interior.at[:, :HB].add(from_below)

    residual = apply_transpose(demand - forward(prior_mean)) - linear_cost[None] - multipliers
    primal = prior_mean

    def squares(values):
        return lax.psum(inner_sum(values, values), "net")

    direction = residual
    norm_now = squares(residual)
    for sweep in range(ITERS):
        curved = penalty[None] * direction + apply_transpose(forward(direction))
        step_size = norm_now / lax.psum(inner_sum(direction, curved), "net")
        primal = primal + step_size[:, None, None] * direction
        residual = residual - step_size[:, None, None] * curved
        if sweep + 1 < ITERS:
            norm_next = squares(residual)
            direction = residual + (norm_next / norm_now)[:, None, None] * direction
            norm_now = norm_next
    clipped = jnp.maximum(primal, 0.0)
    scen_nodes = lax.axis_size("scen")
    scen_total = scen_count * scen_nodes
    total_log = scen_total.bit_length() - 1
    group_log = total_log - block_section
    group_size = jnp.left_shift(jnp.ones_like(group_log), group_log)
    local_log = jnp.minimum(group_log, scen_count.bit_length() - 1)
    local_rows = jnp.arange(scen_count, dtype=jnp.int32)
    mine = jnp.right_shift(local_rows[:, None, None], local_log[None, None, :])
    theirs = jnp.right_shift(local_rows[None, :, None], local_log[None, None, :])
    same_group = (mine == theirs).astype(jnp.float32)
    group_sums = jnp.einsum("stn,tnc->snc", same_group, clipped, precision=exact_mode)
    for bit_pos in range(scen_nodes.bit_length() - 1):
        partner = from_partner(group_sums, "scen", bit_pos)
        include = scen_count << bit_pos < group_size
        group_sums = group_sums + jnp.where(include[None, :, None], partner, 0.0)
    consensus = group_sums / group_size.astype(jnp.float32)[None, :, None]
    new_multipliers = multipliers + penalty[None] * (clipped - consensus)
    return (consensus, new_multipliers)


def solution(mesh):
    placed = (
        P("scen", "net", None),
        P("scen", "net", None),
        P("scen", "net", None),
        P("net", None),
        P("net", None),
        P("net", None, None, None),
        P("net", None),
        P("net"),
    )
    return jax.shard_map(
        body,
        mesh=mesh,
        in_specs=placed,
        out_specs=(P("scen", "net", None), P("scen", "net", None)),
        check_vma=False,
    )
```

profile of v0, /device:TPU:0, one launch (start us, length us, event | category | flops | bytes accessed | tf_op | source)
XLA Modules:
  0.0 83.2 jit_solution(11469626794003152351)
XLA Ops:
  1.5 2.5 %collective-permute-start = (f32[4,2,128]{2,1,0:T(2,128)S(1)}, f32[4,2,128]{2,1,0:T(2,128)S(1)}, u32[]{:S(2)}, u32[]{:S(2)}) collective-permute-start(f32[4,2,128]{2,1,0:T(2,128)S(1)} %get-tuple-element.90), channel_id=1, source_target_pairs={{0,1},{2,3},{4,5},{6,7},{8,9},{10,11},{12,13},{14,15},{16,17},{18,... | collective-permute-start | bytes 12296 | tf_op jit(solution)/shard_map/ppermute | solution.py:18
  5.4 1.8 %collective-permute-done.1 = f32[4,2,128]{2,1,0:T(2,128)S(1)} collective-permute-done((f32[4,2,128]{2,1,0:T(2,128)S(1)}, f32[4,2,128]{2,1,0:T(2,128)S(1)}, u32[]{:S(2)}, u32[]{:S(2)}) %collective-permute-start.1) | collective-permute-done | bytes 4128 | tf_op jit(solution)/shard_map/ppermute | solution.py:21
  8.2 5.3 %fusion.1 = f32[4,16,128,1]{2,0,3,1:T(4,128)S(1)} fusion(f32[16,4,128,128]{3,2,1,0:T(8,128)} %param.25, f32[4,16,4,128]{3,1,2,0:T(8,128)S(1)} %convolution_bitcast_fusion.5, f32[4,16,128]{2,1,0:T(8,128)} %param.22), kind=kOutput, calls=%fused_computation.13 | convolution fusion | flops 50339840 | bytes 4390912 | tf_op jit(solution)/shard_map/ikrc,sikc->sir/dot_general | solution.py:62
  13.5 2.1 %convolution_bitcast_fusion.4 = f32[4,16,4,128]{3,0,2,1:T(4,128)S(1)} fusion(f32[4,16,128,1]{2,0,3,1:T(4,128)S(1)} %fusion.1, f32[16,4,128,128]{3,2,1,0:T(8,128)S(1)} %copy-done), kind=kOutput, calls=%fused_computation.4 | convolution fusion | flops 50331648 | bytes 4358144 | tf_op jit(solution)/shard_map/ikrc,sir->sikc/dot_general | solution.py:65
  17.2 3.0 %collective-permute-start.3 = (f32[4,2,128]{2,1,0:T(2,128)S(1)}, f32[4,2,128]{2,1,0:T(2,128)S(1)}, u32[]{:S(2)}, u32[]{:S(2)}) collective-permute-start(f32[4,2,128]{2,1,0:T(2,128)S(1)} %get-tuple-element.84), channel_id=1, source_target_pairs={{0,1},{2,3},{4,5},{6,7},{8,9},{10,11},{12,13},{14,15},{16,17},{18,... | collective-permute-start | bytes 12296 | tf_op jit(solution)/shard_map/ppermute | solution.py:29
  21.1 2.2 %collective-permute-start.4 = (f32[4,2,128]{2,1,0:T(2,128)S(1)}, f32[4,2,128]{2,1,0:T(2,128)S(1)}, u32[]{:S(2)}, u32[]{:S(2)}) collective-permute-start(f32[4,2,128]{2,1,0:T(2,128)S(1)} %get-tuple-element.88), channel_id=1, source_target_pairs={{0,1},{2,3},{4,5},{6,7},{8,9},{10,11},{12,13},{14,15},{16,17},{18,... | collective-permute-start | bytes 12296 | tf_op jit(solution)/shard_map/ppermute | solution.py:18
  26.7 3.6 %convolution_bitcast_fusion.10 = f32[4,16,128,1]{2,0,3,1:T(4,128)S(1)} fusion(f32[16,4,128,128]{3,2,1,0:T(8,128)S(1)} %copy-done, f32[4,16,4,128]{3,1,2,0:T(8,128)S(1)} %convolution_bitcast_fusion.3), kind=kOutput, calls=%fused_computation.10 | convolution fusion | flops 50331648 | bytes 4358144 | tf_op jit(solution)/shard_map/ikrc,sikc->sir/dot_general | solution.py:62
  30.3 2.1 %convolution_bitcast_fusion.2 = f32[4,16,4,128]{3,0,2,1:T(4,128)S(1)} fusion(f32[4,16,128,1]{2,0,3,1:T(4,128)S(1)} %convolution_bitcast_fusion.10, f32[16,4,128,128]{3,2,1,0:T(8,128)S(1)} %copy-done), kind=kOutput, calls=%fused_computation.2 | convolution fusion | flops 50331648 | bytes 4358144 | tf_op jit(solution)/shard_map/ikrc,sir->sikc/dot_general | solution.py:65
  34.0 3.0 %collective-permute-start.7 = (f32[4,2,128]{2,1,0:T(2,128)S(1)}, f32[4,2,128]{2,1,0:T(2,128)S(1)}, u32[]{:S(2)}, u32[]{:S(2)}) collective-permute-start(f32[4,2,128]{2,1,0:T(2,128)S(1)} %get-tuple-element.82), channel_id=1, source_target_pairs={{0,1},{2,3},{4,5},{6,7},{8,9},{10,11},{12,13},{14,15},{16,17},{18,... | collective-permute-start | bytes 12296 | tf_op jit(solution)/shard_map/ppermute | solution.py:29
  38.0 2.5 %all-reduce = (f32[4]{0:T(128)S(1)}, f32[4]{0:T(128)S(1)}) all-reduce(f32[4]{0:T(128)S(1)} %get-tuple-element.75, f32[4]{0:T(128)S(1)} %get-tuple-element.74), channel_id=1, replica_groups=mesh['scen'=16,'net'=2] {'net'}, use_global_device_ids=true, to_apply=%region_1.0 | all-reduce | flops 8 | bytes 64 | tf_op jit(solution)/shard_map/psum | solution.py:77
  40.6 2.5 %psum.30 = f32[4]{0:T(128)S(1)} all-reduce(f32[4]{0:T(128)S(1)} %multiply_reduce_fusion.1), channel_id=1, replica_groups=mesh['scen'=16,'net'=2] {'net'}, use_global_device_ids=true, to_apply=%region_5.0 | all-reduce | flops 4 | bytes 32 | tf_op jit(solution)/shard_map/psum | solution.py:77
  43.2 2.5 %collective-permute-start.8 = (f32[4,2,128]{2,1,0:T(2,128)S(1)}, f32[4,2,128]{2,1,0:T(2,128)S(1)}, u32[]{:S(2)}, u32[]{:S(2)}) collective-permute-start(f32[4,2,128]{2,1,0:T(2,128)S(1)} %get-tuple-element.86), channel_id=1, source_target_pairs={{0,1},{2,3},{4,5},{6,7},{8,9},{10,11},{12,13},{14,15},{16,17},{18,... | collective-permute-start | bytes 12296 | tf_op jit(solution)/shard_map/ppermute | solution.py:18
  49.1 5.3 %convolution_bitcast_fusion.9 = f32[4,16,128,1]{2,0,3,1:T(4,128)S(1)} fusion(f32[16,4,128,128]{3,2,1,0:T(8,128)} %param.25, f32[4,16,4,128]{3,1,2,0:T(8,128)S(1)} %convolution_bitcast_fusion.1), kind=kOutput, calls=%fused_computation.9 | convolution fusion | flops 50331648 | bytes 4358144 | tf_op jit(solution)/shard_map/ikrc,sikc->sir/dot_general | solution.py:62
  54.4 2.1 %convolution_bitcast_fusion = f32[4,16,4,128]{3,0,2,1:T(4,128)S(1)} fusion(f32[4,16,128,1]{2,0,3,1:T(4,128)S(1)} %convolution_bitcast_fusion.9, f32[16,4,128,128]{3,2,1,0:T(8,128)S(1)} %copy-done.1), kind=kOutput, calls=%fused_computation | convolution fusion | flops 50331648 | bytes 4358144 | tf_op jit(solution)/shard_map/ikrc,sir->sikc/dot_general | solution.py:65
  58.1 3.0 %collective-permute-start.11 = (f32[4,2,128]{2,1,0:T(2,128)S(1)}, f32[4,2,128]{2,1,0:T(2,128)S(1)}, u32[]{:S(2)}, u32[]{:S(2)}) collective-permute-start(f32[4,2,128]{2,1,0:T(2,128)S(1)} %get-tuple-element.80), channel_id=1, source_target_pairs={{0,1},{2,3},{4,5},{6,7},{8,9},{10,11},{12,13},{14,15},{16,17},{18,... | collective-permute-start | bytes 12296 | tf_op jit(solution)/shard_map/ppermute | solution.py:29
  62.2 2.5 %psum.31 = f32[4]{0:T(128)S(1)} all-reduce(f32[4]{0:T(128)S(1)} %multiply_reduce_fusion), channel_id=1, replica_groups=mesh['scen'=16,'net'=2] {'net'}, use_global_device_ids=true, to_apply=%region_7.0 | all-reduce | flops 4 | bytes 32 | tf_op jit(solution)/shard_map/psum | solution.py:83
  65.0 2.4 %collective-permute-start.12 = (f32[4,16,128]{2,1,0:T(8,128)S(1)}, f32[4,16,128]{2,1,0:T(8,128)S(1)}, u32[]{:S(2)}, u32[]{:S(2)}) collective-permute-start(f32[4,16,128]{2,1,0:T(8,128)S(1)} %bitcast.95), channel_id=1, source_target_pairs={{0,2},{2,0},{4,6},{6,4},{8,10},{10,8},{12,14},{14,12},{16,18},{18,... | collective-permute-start | bytes 98312 | tf_op jit(solution)/shard_map/ppermute | solution.py:35
  67.4 1.9 %collective-permute-done.12 = f32[4,16,128]{2,1,0:T(8,128)S(1)} collective-permute-done((f32[4,16,128]{2,1,0:T(8,128)S(1)}, f32[4,16,128]{2,1,0:T(8,128)S(1)}, u32[]{:S(2)}, u32[]{:S(2)}) %collective-permute-start.12) | collective-permute-done | bytes 32800 | tf_op jit(solution)/shard_map/ppermute | solution.py:35
  69.3 2.0 %collective-permute-start.13 = (f32[4,16,128]{2,1,0:T(8,128)S(1)}, f32[4,16,128]{2,1,0:T(8,128)S(1)}, u32[]{:S(2)}, u32[]{:S(2)}) collective-permute-start(f32[4,16,128]{2,1,0:T(8,128)S(1)} %select_add_fusion.2), channel_id=1, source_target_pairs={{0,4},{2,6},{4,0},{6,2},{8,12},{10,14},{12,8},{14,10},{16,20},{18,... | collective-permute-start | bytes 98312 | tf_op jit(solution)/shard_map/ppermute | solution.py:35
  71.4 1.9 %collective-permute-done.13 = f32[4,16,128]{2,1,0:T(8,128)S(1)} collective-permute-done((f32[4,16,128]{2,1,0:T(8,128)S(1)}, f32[4,16,128]{2,1,0:T(8,128)S(1)}, u32[]{:S(2)}, u32[]{:S(2)}) %collective-permute-start.13) | collective-permute-done | bytes 32800 | tf_op jit(solution)/shard_map/ppermute | solution.py:35
  73.3 2.1 %collective-permute-start.14 = (f32[4,16,128]{2,1,0:T(8,128)S(1)}, f32[4,16,128]{2,1,0:T(8,128)S(1)}, u32[]{:S(2)}, u32[]{:S(2)}) collective-permute-start(f32[4,16,128]{2,1,0:T(8,128)S(1)} %select_add_fusion.1), channel_id=1, source_target_pairs={{0,8},{2,10},{4,12},{6,14},{8,0},{10,2},{12,4},{14,6},{16,24},{18,... | collective-permute-start | bytes 98312 | tf_op jit(solution)/shard_map/ppermute | solution.py:35
  75.4 1.9 %collective-permute-done.14 = f32[4,16,128]{2,1,0:T(8,128)S(1)} collective-permute-done((f32[4,16,128]{2,1,0:T(8,128)S(1)}, f32[4,16,128]{2,1,0:T(8,128)S(1)}, u32[]{:S(2)}, u32[]{:S(2)}) %collective-permute-start.14) | collective-permute-done | bytes 32800 | tf_op jit(solution)/shard_map/ppermute | solution.py:35
  77.4 3.2 %collective-permute-start.15 = (f32[4,16,128]{2,1,0:T(8,128)S(1)}, f32[4,16,128]{2,1,0:T(8,128)S(1)}, u32[]{:S(2)}, u32[]{:S(2)}) collective-permute-start(f32[4,16,128]{2,1,0:T(8,128)S(1)} %select_add_fusion), channel_id=1, source_target_pairs={{0,16},{2,18},{4,20},{6,22},{8,24},{10,26},{12,28},{14,30},{16,0},... | collective-permute-start | bytes 98312 | tf_op jit(solution)/shard_map/ppermute | solution.py:35
  80.6 1.9 %collective-permute-done.15 = f32[4,16,128]{2,1,0:T(8,128)S(1)} collective-permute-done((f32[4,16,128]{2,1,0:T(8,128)S(1)}, f32[4,16,128]{2,1,0:T(8,128)S(1)}, u32[]{:S(2)}, u32[]{:S(2)}) %collective-permute-start.15) | collective-permute-done | bytes 32800 | tf_op jit(solution)/shard_map/ppermute | solution.py:35
  (72 shorter events, 18.9 us)
Async XLA Ops:
  0.6 12.9 %copy-start = (f32[16,4,128,128]{3,2,1,0:T(8,128)S(1)}, f32[16,4,128,128]{3,2,1,0:T(8,128)}, u32[]{:S(2)}) copy-start(f32[16,4,128,128]{3,2,1,0:T(8,128)} %param.25) | copy-start | bytes 12582916
  1.5 3.8 %collective-permute-start = (f32[4,2,128]{2,1,0:T(2,128)S(1)}, f32[4,2,128]{2,1,0:T(2,128)S(1)}, u32[]{:S(2)}, u32[]{:S(2)}) collective-permute-start(f32[4,2,128]{2,1,0:T(2,128)S(1)} %get-tuple-element.90), channel_id=1, source_target_pairs={{0,1},{2,3},{4,5},{6,7},{8,9},{10,11},{12,13},{14,15},{16,17},{18,... | collective-permute-start | bytes 12296 | tf_op jit(solution)/shard_map/ppermute | solution.py:18
  4.1 3.1 %collective-permute-start.1 = (f32[4,2,128]{2,1,0:T(2,128)S(1)}, f32[4,2,128]{2,1,0:T(2,128)S(1)}, u32[]{:S(2)}, u32[]{:S(2)}) collective-permute-start(f32[4,2,128]{2,1,0:T(2,128)S(1)} %get-tuple-element.91), channel_id=1, source_target_pairs={{1,0},{3,2},{5,4},{7,6},{9,8},{11,10},{13,12},{15,14},{17,16},{19,... | collective-permute-start | bytes 12296 | tf_op jit(solution)/shard_map/ppermute | solution.py:21
  8.1 7.5 %copy-start.5 = (s32[16,4]{0,1:T(4,128)S(1)}, s32[16,4]{0,1:T(4,128)}, u32[]{:S(2)}) copy-start(s32[16,4]{0,1:T(4,128)} %param.26) | copy-start | bytes 772
  8.1 12.9 %copy-start.4 = (f32[4,16,128]{2,1,0:T(8,128)S(1)}, f32[4,16,128]{2,1,0:T(8,128)}, u32[]{:S(2)}) copy-start(f32[4,16,128]{2,1,0:T(8,128)} %param.21) | copy-start | bytes 98308
  8.2 12.9 %copy-start.6 = (f32[16,128]{1,0:T(8,128)S(1)}, f32[16,128]{1,0:T(8,128)}, u32[]{:S(2)}) copy-start(f32[16,128]{1,0:T(8,128)} %param.23) | copy-start | bytes 24580
  15.9 4.4 %collective-permute-start.2 = (f32[4,2,128]{2,1,0:T(2,128)S(1)}, f32[4,2,128]{2,1,0:T(2,128)S(1)}, u32[]{:S(2)}, u32[]{:S(2)}) collective-permute-start(f32[4,2,128]{2,1,0:T(2,128)S(1)} %get-tuple-element.85), channel_id=1, source_target_pairs={{1,0},{3,2},{5,4},{7,6},{9,8},{11,10},{13,12},{15,14},{17,16},{19,... | collective-permute-start | bytes 12296 | tf_op jit(solution)/shard_map/ppermute | solution.py:29
  17.2 3.8 %collective-permute-start.3 = (f32[4,2,128]{2,1,0:T(2,128)S(1)}, f32[4,2,128]{2,1,0:T(2,128)S(1)}, u32[]{:S(2)}, u32[]{:S(2)}) collective-permute-start(f32[4,2,128]{2,1,0:T(2,128)S(1)} %get-tuple-element.84), channel_id=1, source_target_pairs={{0,1},{2,3},{4,5},{6,7},{8,9},{10,11},{12,13},{14,15},{16,17},{18,... | collective-permute-start | bytes 12296 | tf_op jit(solution)/shard_map/ppermute | solution.py:29
  21.1 3.6 %collective-permute-start.4 = (f32[4,2,128]{2,1,0:T(2,128)S(1)}, f32[4,2,128]{2,1,0:T(2,128)S(1)}, u32[]{:S(2)}, u32[]{:S(2)}) collective-permute-start(f32[4,2,128]{2,1,0:T(2,128)S(1)} %get-tuple-element.88), channel_id=1, source_target_pairs={{0,1},{2,3},{4,5},{6,7},{8,9},{10,11},{12,13},{14,15},{16,17},{18,... | collective-permute-start | bytes 12296 | tf_op jit(solution)/shard_map/ppermute | solution.py:18
  23.4 3.1 %collective-permute-start.5 = (f32[4,2,128]{2,1,0:T(2,128)S(1)}, f32[4,2,128]{2,1,0:T(2,128)S(1)}, u32[]{:S(2)}, u32[]{:S(2)}) collective-permute-start(f32[4,2,128]{2,1,0:T(2,128)S(1)} %get-tuple-element.89), channel_id=1, source_target_pairs={{1,0},{3,2},{5,4},{7,6},{9,8},{11,10},{13,12},{15,14},{17,16},{19,... | collective-permute-start | bytes 12296 | tf_op jit(solution)/shard_map/ppermute | solution.py:21
  26.7 11.2 %copy-start.2 = (f32[16,128]{1,0:T(8,128)S(1)}, f32[16,128]{1,0:T(8,128)}, u32[]{:S(2)}) copy-start(f32[16,128]{1,0:T(8,128)} %param.24) | copy-start | bytes 24580
  32.7 4.4 %collective-permute-start.6 = (f32[4,2,128]{2,1,0:T(2,128)S(1)}, f32[4,2,128]{2,1,0:T(2,128)S(1)}, u32[]{:S(2)}, u32[]{:S(2)}) collective-permute-start(f32[4,2,128]{2,1,0:T(2,128)S(1)} %get-tuple-element.83), channel_id=1, source_target_pairs={{1,0},{3,2},{5,4},{7,6},{9,8},{11,10},{13,12},{15,14},{17,16},{19,... | collective-permute-start | bytes 12296 | tf_op jit(solution)/shard_map/ppermute | solution.py:29
  34.0 3.8 %collective-permute-start.7 = (f32[4,2,128]{2,1,0:T(2,128)S(1)}, f32[4,2,128]{2,1,0:T(2,128)S(1)}, u32[]{:S(2)}, u32[]{:S(2)}) collective-permute-start(f32[4,2,128]{2,1,0:T(2,128)S(1)} %get-tuple-element.82), channel_id=1, source_target_pairs={{0,1},{2,3},{4,5},{6,7},{8,9},{10,11},{12,13},{14,15},{16,17},{18,... | collective-permute-start | bytes 12296 | tf_op jit(solution)/shard_map/ppermute | solution.py:29
  43.1 11.3 %copy-start.1 = (f32[16,4,128,128]{3,2,1,0:T(8,128)S(1)}, f32[16,4,128,128]{3,2,1,0:T(8,128)}, u32[]{:S(2)}) copy-start(f32[16,4,128,128]{3,2,1,0:T(8,128)} %param.25) | copy-start | bytes 12582916
  43.2 4.0 %collective-permute-start.8 = (f32[4,2,128]{2,1,0:T(2,128)S(1)}, f32[4,2,128]{2,1,0:T(2,128)S(1)}, u32[]{:S(2)}, u32[]{:S(2)}) collective-permute-start(f32[4,2,128]{2,1,0:T(2,128)S(1)} %get-tuple-element.86), channel_id=1, source_target_pairs={{0,1},{2,3},{4,5},{6,7},{8,9},{10,11},{12,13},{14,15},{16,17},{18,... | collective-permute-start | bytes 12296 | tf_op jit(solution)/shard_map/ppermute | solution.py:18
  45.7 3.1 %collective-permute-start.9 = (f32[4,2,128]{2,1,0:T(2,128)S(1)}, f32[4,2,128]{2,1,0:T(2,128)S(1)}, u32[]{:S(2)}, u32[]{:S(2)}) collective-permute-start(f32[4,2,128]{2,1,0:T(2,128)S(1)} %get-tuple-element.87), channel_id=1, source_target_pairs={{1,0},{3,2},{5,4},{7,6},{9,8},{11,10},{13,12},{15,14},{17,16},{19,... | collective-permute-start | bytes 12296 | tf_op jit(solution)/shard_map/ppermute | solution.py:21
  49.0 9.0 %copy-start.7 = (s32[16]{0:T(128)S(1)}, s32[16]{0:T(128)}, u32[]{:S(2)}) copy-start(s32[16]{0:T(128)} %param.27) | copy-start | bytes 196
  49.1 15.6 %copy-start.3 = (f32[4,16,128]{2,1,0:T(8,128)S(1)}, f32[4,16,128]{2,1,0:T(8,128)}, u32[]{:S(2)}) copy-start(f32[4,16,128]{2,1,0:T(8,128)} %param.20) | copy-start | bytes 98308
  56.8 4.4 %collective-permute-start.10 = (f32[4,2,128]{2,1,0:T(2,128)S(1)}, f32[4,2,128]{2,1,0:T(2,128)S(1)}, u32[]{:S(2)}, u32[]{:S(2)}) collective-permute-start(f32[4,2,128]{2,1,0:T(2,128)S(1)} %get-tuple-element.81), channel_id=1, source_target_pairs={{1,0},{3,2},{5,4},{7,6},{9,8},{11,10},{13,12},{15,14},{17,16},{19,... | collective-permute-start | bytes 12296 | tf_op jit(solution)/shard_map/ppermute | solution.py:29
  58.1 3.8 %collective-permute-start.11 = (f32[4,2,128]{2,1,0:T(2,128)S(1)}, f32[4,2,128]{2,1,0:T(2,128)S(1)}, u32[]{:S(2)}, u32[]{:S(2)}) collective-permute-start(f32[4,2,128]{2,1,0:T(2,128)S(1)} %get-tuple-element.80), channel_id=1, source_target_pairs={{0,1},{2,3},{4,5},{6,7},{8,9},{10,11},{12,13},{14,15},{16,17},{18,... | collective-permute-start | bytes 12296 | tf_op jit(solution)/shard_map/ppermute | solution.py:29
  65.0 4.3 %collective-permute-start.12 = (f32[4,16,128]{2,1,0:T(8,128)S(1)}, f32[4,16,128]{2,1,0:T(8,128)S(1)}, u32[]{:S(2)}, u32[]{:S(2)}) collective-permute-start(f32[4,16,128]{2,1,0:T(8,128)S(1)} %bitcast.95), channel_id=1, source_target_pairs={{0,2},{2,0},{4,6},{6,4},{8,10},{10,8},{12,14},{14,12},{16,18},{18,... | collective-permute-start | bytes 98312 | tf_op jit(solution)/shard_map/ppermute | solution.py:35
  69.3 3.9 %collective-permute-start.13 = (f32[4,16,128]{2,1,0:T(8,128)S(1)}, f32[4,16,128]{2,1,0:T(8,128)S(1)}, u32[]{:S(2)}, u32[]{:S(2)}) collective-permute-start(f32[4,16,128]{2,1,0:T(8,128)S(1)} %select_add_fusion.2), channel_id=1, source_target_pairs={{0,4},{2,6},{4,0},{6,2},{8,12},{10,14},{12,8},{14,10},{16,20},{18,... | collective-permute-start | bytes 98312 | tf_op jit(solution)/shard_map/ppermute | solution.py:35
  73.3 4.0 %collective-permute-start.14 = (f32[4,16,128]{2,1,0:T(8,128)S(1)}, f32[4,16,128]{2,1,0:T(8,128)S(1)}, u32[]{:S(2)}, u32[]{:S(2)}) collective-permute-start(f32[4,16,128]{2,1,0:T(8,128)S(1)} %select_add_fusion.1), channel_id=1, source_target_pairs={{0,8},{2,10},{4,12},{6,14},{8,0},{10,2},{12,4},{14,6},{16,24},{18,... | collective-permute-start | bytes 98312 | tf_op jit(solution)/shard_map/ppermute | solution.py:35
  77.4 5.1 %collective-permute-start.15 = (f32[4,16,128]{2,1,0:T(8,128)S(1)}, f32[4,16,128]{2,1,0:T(8,128)S(1)}, u32[]{:S(2)}, u32[]{:S(2)}) collective-permute-start(f32[4,16,128]{2,1,0:T(8,128)S(1)} %select_add_fusion), channel_id=1, source_target_pairs={{0,16},{2,18},{4,20},{6,22},{8,24},{10,26},{12,28},{14,30},{16,0},... | collective-permute-start | bytes 98312 | tf_op jit(solution)/shard_map/ppermute | solution.py:35
where the time goes:
time: 83.6 us; the launch traced here: 83.2 us
  starting transfers between devices  34 us (41%)
  matrix products  23.1 us (28%)
  waiting for transfers between devices  15 us (18%)
  blocking collectives  7.39 us (9%)
  other arithmetic  1.69 us (2%)
  between operations  1.03 us (1%)
  local copies, waits for them, and re-layouts  1 us (1%)
    dot_general x3, matrix products, forward(): jnp.einsum('ikrc,sikc->sir', constraint_blocks, picked, precision=exact_m...  14.2 us
    ppermute x6, starting transfers between devices, shifted(): return lax.ppermute(block, axis, route)  13 us
    ppermute x4, starting transfers between devices, from_partner(): return lax.ppermute(value, axis, pairs)  9.69 us
    ppermute x4, waiting for transfers between devices, from_partner(): return lax.ppermute(value, axis, pairs)  7.57 us
    ppermute x3, starting transfers between devices, extended_2(): lax.ppermute(lax.slice_in_dim(block, block.shape[dim] - width, None, axis...  7.28 us
    dot_general x3, matrix products, apply_transpose(): jnp.einsum('ikrc,sir->sikc', constraint_blocks, values, precision=exact_m...  6.27 us
    ppermute x3, waiting for transfers between devices, extended_2(): lax.ppermute(lax.slice_in_dim(block, 0, width, axis=dim), axis, backward)  5.07 us
    psum x2, blocking collectives, squares(): return lax.psum(inner_sum(values, values), 'net')  4.94 us
  transfers between devices with their start and end apart: 16, of which 10 were waited for; matrix products, arithmetic and copies ran while one was open for 0% of the time, Pallas kernels for 0%

commit v1 on v0

v1 whole, which is shorter than its diff:
```python
import functools

import jax
import jax.numpy as jnp
from jax import lax
from jax.experimental import pallas as pl
from jax.experimental.pallas import tpu as pltpu
from jax.sharding import PartitionSpec as P

HB = 2
MESH = pl.DeviceIdType.MESH


def phases_of(nodes):
    bits = nodes.bit_length() - 1
    out = []
    at = 0
    while at < bits:
        take = min(2, bits - at)
        out.append((at, [m << at for m in range(1, 1 << take)]))
        at += take
    return out


def kernel(
    nets,
    nodes,
    x_hbm,
    lam_hbm,
    dem_hbm,
    cost_hbm,
    pen_hbm,
    mat_hbm,
    col_hbm,
    sec_hbm,
    cons_ref,
    newm_ref,
    x_in,
    lam_in,
    dem_in,
    cost_in,
    pen_in,
    mat_in,
    cols,
    secs,
    split,
    xv,
    bv,
    dv,
    penb,
    hl,
    rv,
    w0,
    sec_rows,
    x_got,
    msg_out,
    msg_in,
    sum_out,
    sum_in,
    in_sem,
    mat_sem,
    xs_sem,
    xr_sem,
    ms_sem,
    mr_sem,
    ss_sem,
    sr_sem,
):
    L, nb, blk = x_in.shape
    nnz = mat_in.shape[1]
    R = 2 * L
    me_s = lax.axis_index("scen")
    me_n = lax.axis_index("net")
    phases = phases_of(nodes)

    small = [
        pltpu.make_async_copy(src, dst, in_sem.at[j])
        for j, (src, dst) in enumerate(
            [
                (x_hbm, x_in),
                (col_hbm, cols),
                (dem_hbm, dem_in),
                (lam_hbm, lam_in),
                (cost_hbm, cost_in),
                (pen_hbm, pen_in),
                (sec_hbm, secs),
            ]
        )
    ]
    for copy in small:
        copy.start()
    mats = [pltpu.make_async_copy(mat_hbm.at[i], mat_in.at[i], mat_sem.at[i]) for i in range(nb)]
    for copy in mats:
        copy.start()

    net_peer = [lax.rem(me_n + p, nets) for p in range(1, nets)]
    barrier = pltpu.get_barrier_semaphore()
    count = 0
    for peer in net_peer:
        pl.semaphore_signal(barrier, inc=1, device_id=(me_s, peer), device_id_type=MESH)
        count += 1

    def scen_peer(at, mask):
        bit = mask >> at
        low = lax.rem(me_s // (1 << at), 2)
        flipped = me_s
        if bit & 1:
            flipped = flipped + (1 - 2 * low) * (1 << at)
        if bit & 2:
            high = lax.rem(me_s // (2 << at), 2)
            flipped = flipped + (1 - 2 * high) * (2 << at)
        return flipped

    for at, masks in phases:
        for mask in masks:
            pl.semaphore_signal(
                barrier, inc=1, device_id=(scen_peer(at, mask), me_n), device_id_type=MESH
            )
            count += 1

    has_left = me_n > 0
    has_right = me_n < nets - 1

    def make_split(i):
        for k in range(nnz):
            a = mat_in[i, k]
            hi = a.astype(jnp.bfloat16)
            split[i, 0:blk, k * blk : (k + 1) * blk] = hi
            split[i, blk : 2 * blk, k * blk : (k + 1) * blk] = (
                a - hi.astype(jnp.float32)
            ).astype(jnp.bfloat16)

    first_half = nb // 2

    @pl.loop(0, first_half)
    def _(i):
        pltpu.make_async_copy(mat_hbm.at[i], mat_in.at[i], mat_sem.at[i]).wait()
        make_split(i)

    pl.semaphore_wait(barrier, count)
    x_sends = [
        pltpu.make_async_remote_copy(
            src_ref=x_hbm,
            dst_ref=x_got.at[p],
            send_sem=xs_sem.at[p],
            recv_sem=xr_sem.at[p],
            device_id=(me_s, peer),
            device_id_type=MESH,
        )
        for p, peer in enumerate(net_peer)
    ]
    for copy in x_sends:
        copy.start()
    for copy in small:
        copy.wait()

    upper = lax.broadcasted_iota(jnp.int32, (R, blk), 0) < L

    def halves(v):
        hi = v.astype(jnp.bfloat16).astype(jnp.float32)
        return jnp.where(upper, hi, v - hi)

    for s in range(L):
        for r in (s, s + L):
            xv[pl.ds(r, nb, stride=R), :] = x_in[s]
            bv[pl.ds(r, nb, stride=R), :] = dem_in[s]
            dv[pl.ds(r, nb, stride=R), :] = cost_in[...] + lam_in[s]
            penb[pl.ds(r, nb, stride=R), :] = pen_in[...]
    for i in range(nb):
        sec_rows[i : i + 1, :] = jnp.full((1, blk), secs[i], jnp.int32)
        hl[HB + i] = halves(xv[i * R : (i + 1) * R, :])

    @pl.loop(first_half, nb)
    def _(i):
        pltpu.make_async_copy(mat_hbm.at[i], mat_in.at[i], mat_sem.at[i]).wait()
        make_split(i)

    for copy in x_sends:
        copy.wait()

    def halo_of_rows(ref, rows):
        return [
            jnp.concatenate([ref[s, r : r + 1] for s in list(range(L)) * 2], axis=0) for r in rows
        ]

    zero = jnp.zeros((R, blk), jnp.float32)

    def set_halo(low, high):
        for j in range(HB):
            hl[j] = halves(jnp.where(has_left, low[j], zero))
            hl[HB + nb + j] = halves(jnp.where(has_right, high[j], zero))

    if nets > 1:
        set_halo(
            halo_of_rows(x_got.at[0], range(nb - HB, nb)),
            halo_of_rows(x_got.at[nets - 2], range(HB)),
        )
    else:
        set_halo([zero] * HB, [zero] * HB)

    def forward_row(i):
        lhs = jnp.concatenate([hl[cols[i, k]] for k in range(nnz)], axis=1).astype(jnp.bfloat16)
        out = lax.dot_general(
            lhs, split[i], (((1,), (1,)), ((), ())), preferred_element_type=jnp.float32
        )
        both = out[:, :blk] + out[:, blk:]
        return both + pltpu.roll(both, L, 0)

    def transpose_row(i, w, acc):
        h = halves(w)
        lhs = jnp.concatenate([h, h], axis=1).astype(jnp.bfloat16)
        out = lax.dot_general(
            lhs, split[i], (((1,), (0,)), ((), ())), preferred_element_type=jnp.float32
        )
        both = out + pltpu.roll(out, L, 0)

        def put(at, term):
            acc[at] = term if acc[at] is None else acc[at] + term

        put(HB + i, both[:, :blk])
        for k in range(1, nnz):
            term = both[:, k * blk : (k + 1) * blk]
            for o in range(-HB, HB + 1):
                if o != 0:
                    put(HB + i + o, jnp.where(cols[i, k] == HB + i + o, term, zero))

    edge = list(range(HB)) + list(range(nb - HB, nb))
    inner = list(range(HB, nb - HB))

    def send(e, blocks, partial):
        for j, b in enumerate(blocks):
            if b is not None:
                msg_out[e, j] = b
        if partial is not None:
            msg_out[e, 2 * HB] = partial
        first = 0 if blocks else 2 * HB
        last = 2 * HB + (1 if partial is not None else 0)
        copies = [
            pltpu.make_async_remote_copy(
                src_ref=msg_out.at[e, pl.ds(first, last - first)],
                dst_ref=msg_in.at[e, p, pl.ds(first, last - first)],
                send_sem=ms_sem.at[e, p],
                recv_sem=mr_sem.at[e, p],
                device_id=(me_s, peer),
                device_id_type=MESH,
            )
            for p, peer in enumerate(net_peer)
        ]
        for copy in copies:
            copy.start()
        return copies

    def neighbours(e):
        if nets == 1:
            return [zero] * HB, [zero] * HB
        low = [jnp.where(has_left, msg_in[e, 0, HB + j], zero) for j in range(HB)]
        high = [jnp.where(has_right, msg_in[e, nets - 2, j], zero) for j in range(HB)]
        return low, high

    def total(e, partial):
        for p in range(nets - 1):
            partial = partial + msg_in[e, p, 2 * HB]
        return jnp.sum(partial, axis=1, keepdims=True)

    def wait(copies):
        for copy in copies:
            copy.wait()

    def transposed(e, w, partial):
        acc = [None] * (nb + 2 * HB)
        for i in edge:
            transpose_row(i, w[i], acc)
        copies = send(e, acc[:HB] + acc[HB + nb :], partial)
        for i in inner:
            transpose_row(i, w[i], acc)
        wait(copies)
        low, high = neighbours(e)
        z = acc[HB : HB + nb]
        for j in range(HB):
            z[j] = z[j] + low[j]
            z[nb - HB + j] = z[nb - HB + j] + high[j]
        return z

    def forward_with_halo(e, v, partial):
        copies = send(e, v[:HB] + v[nb - HB :], partial)
        for i in range(nb):
            hl[HB + i] = halves(v[i])
        w = [None] * nb
        for i in inner:
            w[i] = forward_row(i)
        wait(copies)
        low, high = neighbours(e)
        set_halo(low, high)
        for i in edge:
            w[i] = forward_row(i)
        return w

    def rows(ref):
        return [ref[i * R : (i + 1) * R, :] for i in range(nb)]

    def add_all(terms):
        while len(terms) > 1:
            terms = [
                terms[j] + terms[j + 1] if j + 1 < len(terms) else terms[j]
                for j in range(0, len(terms), 2)
            ]
        return terms[0]

    w = [bv[i * R : (i + 1) * R, :] - forward_row(i) for i in range(nb)]
    z = transposed(0, w, None)
    r0 = [z[i] - dv[i * R : (i + 1) * R, :] for i in range(nb)]
    part0 = add_all([v * v for v in r0])
    for i in range(nb):
        rv[i * R : (i + 1) * R, :] = r0[i]
    wa = forward_with_halo(1, r0, part0)
    norm0 = total(1, part0)
    for i in range(nb):
        w0[i * R : (i + 1) * R, :] = wa[i]
    pen = rows(penb)
    part_q = add_all(
        [p * v * v for p, v in zip(pen, rows(rv))] + [v * v for v in wa]
    )
    z = transposed(2, wa, part_q)
    a0 = norm0 / total(2, part_q)
    r0 = rows(rv)
    pen = rows(penb)
    r1 = [r0[i] - a0 * (pen[i] * r0[i] + z[i]) for i in range(nb)]
    part1 = add_all([v * v for v in r1])
    for i in range(nb):
        dv[i * R : (i + 1) * R, :] = r1[i]
        bv[i * R : (i + 1) * R, :] = xv[i * R : (i + 1) * R, :] + a0 * r0[i]
    wb = forward_with_halo(3, r1, part1)
    norm1 = total(3, part1)
    beta = norm1 / norm0
    d1 = [dv[i * R : (i + 1) * R, :] + beta * rv[i * R : (i + 1) * R, :] for i in range(nb)]
    ad = [wb[i] + beta * w0[i * R : (i + 1) * R, :] for i in range(nb)]
    part_q = add_all(
        [penb[i * R : (i + 1) * R, :] * d1[i] * d1[i] for i in range(nb)] + [v * v for v in ad]
    )
    wait(send(4, [], part_q))
    a1 = norm1 / total(4, part_q)
    for i in range(nb):
        rows_i = slice(i * R, (i + 1) * R)
        xv[rows_i, :] = jnp.maximum(bv[rows_i, :] + a1 * d1[i], 0.0)

    clipped = [xv[pl.ds(s, nb, stride=R), :] for s in range(L)]
    group = jnp.right_shift(jnp.int32(L * nodes), sec_rows[...])
    sums = clipped
    for b in range(L.bit_length() - 1):
        sums = [
            sums[s] + jnp.where(group > (1 << b), sums[s ^ (1 << b)], 0.0) for s in range(L)
        ]
    mine = sums[0]
    base = mine
    slot = 0
    for f, (at, masks) in enumerate(phases):
        sum_out[f] = mine
        copies = []
        for j, mask in enumerate(masks):
            copies.append(
                pltpu.make_async_remote_copy(
                    src_ref=sum_out.at[f],
                    dst_ref=sum_in.at[slot + j],
                    send_sem=ss_sem.at[slot + j],
                    recv_sem=sr_sem.at[slot + j],
                    device_id=(scen_peer(at, mask), me_n),
                    device_id_type=MESH,
                )
            )
        for copy in copies:
            copy.start()
        wait(copies)
        got = [sum_in[slot + j] for j in range(len(masks))]
        extra = jnp.where(group > (L << at), got[0], 0.0)
        if len(masks) == 3:
            extra = extra + jnp.where(group > (L << (at + 1)), got[1] + got[2], 0.0)
        mine = mine + extra
        slot += len(masks)
    shared = group >= L
    size = group.astype(jnp.float32)
    for s in range(L):
        mean = jnp.where(shared, mine, sums[s]) / size
        cons_ref[s] = mean
        newm_ref[s] = lam_in[s] + pen_in[...] * (clipped[s] - mean)


def body(*args):
    x = args[0]
    mat = args[5]
    L, nb, blk = x.shape
    nnz = mat.shape[1]
    nets = lax.axis_size("net")
    nodes = lax.axis_size("scen")
    R = 2 * L
    others = max(nets - 1, 1)
    phases = phases_of(nodes)
    slots = max(sum(len(m) for _, m in phases), 1)
    f32 = jnp.float32
    V = pltpu.VMEM
    dma = pltpu.SemaphoreType.DMA
    scratch = [
        V((L, nb, blk), f32),
        V((L, nb, blk), f32),
        V((L, nb, blk), f32),
        V((nb, blk), f32),
        V((nb, blk), f32),
        V(mat.shape, f32),
        pltpu.SMEM((nb, nnz), jnp.int32),
        pltpu.SMEM((nb,), jnp.int32),
        V((nb, 2 * blk, nnz * blk), jnp.bfloat16),
        V((nb * R, blk), f32),
        V((nb * R, blk), f32),
        V((nb * R, blk), f32),
        V((nb * R, blk), f32),
        V((nb + 2 * HB, R, blk), f32),
        V((nb * R, blk), f32),
        V((nb * R, blk), f32),
        V((nb, blk), jnp.int32),
        V((others, L, nb, blk), f32),
        V((5, 2 * HB + 1, R, blk), f32),
        V((5, others, 2 * HB + 1, R, blk), f32),
        V((max(len(phases), 1), nb, blk), f32),
        V((slots, nb, blk), f32),
        dma((7,)),
        dma((nb,)),
        dma((others,)),
        dma((others,)),
        dma((5, others)),
        dma((5, others)),
        dma((slots,)),
        dma((slots,)),
    ]
    any_spec = pl.BlockSpec(memory_space=pl.ANY)
    vmem_spec = pl.BlockSpec(memory_space=pltpu.VMEM)
    return pl.pallas_call(
        functools.partial(kernel, nets, nodes),
        out_shape=(jax.ShapeDtypeStruct(x.shape, f32), jax.ShapeDtypeStruct(x.shape, f32)),
        in_specs=[any_spec] * 8,
        out_specs=(vmem_spec, vmem_spec),
        scratch_shapes=scratch,
        compiler_params=pltpu.CompilerParams(
            collective_id=0, has_side_effects=True, vmem_limit_bytes=40 << 20
        ),
    )(*args)


def solution(mesh):
    placed = (
        P("scen", "net", None),
        P("scen", "net", None),
        P("scen", "net", None),
        P("net", None),
        P("net", None),
        P("net", None, None, None),
        P("net", None),
        P("net"),
    )
    fn = jax.shard_map(
        body,
        mesh=mesh,
        in_specs=placed,
        out_specs=(P("scen", "net", None), P("scen", "net", None)),
        check_vma=False,
    )
    return lambda *args: tuple(fn(*args))
```

time: 83.6 us -> 30.3 us (0.36)
  starting transfers between devices: 34 us -> 0 us
  matrix products: 23.1 us -> 0 us
  Pallas kernels: 0 us -> 20.7 us
  waiting for transfers between devices: 15 us -> 0 us
  local copies, waits for them, and re-layouts: 1 us -> 8.5 us
  blocking collectives: 7.39 us -> 0 us
  other arithmetic: 1.69 us -> 0 us
    ppermute x16 -> x0, starting transfers between devices: 34 us -> none  [the longest x6 13 us: shifted(): return lax.ppermute(block, axis, route)]
    dot_general x13 -> x0, matrix products: 23.1 us -> none  [the longest x3 14.2 us: forward(): jnp.einsum('ikrc,sikc->sir', constraint_blocks, picked, precision=exact_m...]
    pallas_call x0 -> x1, Pallas kernels: none -> 20.7 us  [body(): pl.pallas_call(functools.partial(kernel, nets, nodes), out_shape=(jax.Sha...]
    ppermute x16 -> x0, waiting for transfers between devices: 15 us -> none  [the longest x4 7.57 us: from_partner(): return lax.ppermute(value, axis, pairs)]
    unnamed x16 -> x17, local copies, waits for them, and re-layouts: 0.05 us -> 8.5 us
    psum x3 -> x0, blocking collectives: 7.39 us -> none  [the longest x2 4.94 us: squares(): return lax.psum(inner_sum(values, values), 'net')]
    add x5 -> x0, other arithmetic: 1.01 us -> none  [the longest x1 0.7 us: body(): new_multipliers = multipliers + penalty[None] * (clipped - consensus)]
    slice x9 -> x0, local copies, waits for them, and re-layouts: 0.95 us -> none  [the longest x3 0.91 us: extended_2(): lax.slice_in_dim(block, block.shape[dim] - width, None, axis=dim)]
  transfers between devices with their start and end apart: 16 -> 0, of which waited for: 10 -> 0; matrix products, arithmetic and copies ran while one was open for 0% -> 0% of each run, Pallas kernels for 0% -> 0%
where the time goes in v1:
time: 30.3 us; the launch traced here: 29.8 us
  Pallas kernels  20.7 us (68%)
  local copies, waits for them, and re-layouts  8.5 us (28%)
  between operations  0.65 us (2%)
    pallas_call x1, Pallas kernels, body(): pl.pallas_call(functools.partial(kernel, nets, nodes), out_shape=(jax.Sha...  20.7 us
    unnamed x17, local copies, waits for them, and re-layouts  8.5 us

profile of v1, /device:TPU:0, one launch (start us, length us, event | category | flops | bytes accessed | tf_op | source)
XLA Modules:
  0.0 29.8 jit_solution(16046922820772073434)
XLA Ops:
  0.6 0.8 %copy.10.col_hbm = s32[16,4]{1,0:T(8,128)S(1)} copy(s32[16,4]{0,1:T(4,128)} %param.14) | data formatting | bytes 512 | tf_op args[6]
  1.4 0.0 copy-start
  1.4 2.2 %copy-done = f32[16,4,128,128]{3,2,1,0:T(8,128)S(1)} copy-done((f32[16,4,128,128]{3,2,1,0:T(8,128)S(1)}, f32[16,4,128,128]{3,2,1,0:T(8,128)}, u32[]{:S(2)}) %copy-start) | copy-done | bytes 4194328
  3.6 0.0 copy-start.1
  3.6 0.8 %copy-done.1 = f32[4,16,128]{2,1,0:T(8,128)S(1)} copy-done((f32[4,16,128]{2,1,0:T(8,128)S(1)}, f32[4,16,128]{2,1,0:T(8,128)}, u32[]{:S(2)}) %copy-start.1) | copy-done | bytes 32792
  4.3 0.0 copy-start.2
  4.3 0.8 %copy-done.2 = f32[4,16,128]{2,1,0:T(8,128)S(1)} copy-done((f32[4,16,128]{2,1,0:T(8,128)S(1)}, f32[4,16,128]{2,1,0:T(8,128)}, u32[]{:S(2)}) %copy-start.2) | copy-done | bytes 32792
  5.1 0.0 copy-start.3
  5.1 0.8 %copy-done.3 = f32[4,16,128]{2,1,0:T(8,128)S(1)} copy-done((f32[4,16,128]{2,1,0:T(8,128)S(1)}, f32[4,16,128]{2,1,0:T(8,128)}, u32[]{:S(2)}) %copy-start.3) | copy-done | bytes 32792
  5.9 0.0 copy-start.4
  5.9 0.7 %copy-done.4 = f32[16,128]{1,0:T(8,128)S(1)} copy-done((f32[16,128]{1,0:T(8,128)S(1)}, f32[16,128]{1,0:T(8,128)}, u32[]{:S(2)}) %copy-start.4) | copy-done | bytes 8216
  6.5 0.0 copy-start.5
  6.6 0.7 %copy-done.5 = f32[16,128]{1,0:T(8,128)S(1)} copy-done((f32[16,128]{1,0:T(8,128)S(1)}, f32[16,128]{1,0:T(8,128)}, u32[]{:S(2)}) %copy-start.5) | copy-done | bytes 8216
  7.2 0.0 copy-start.6
  7.2 0.7 %copy-done.6 = s32[16]{0:T(128)S(1)} copy-done((s32[16]{0:T(128)S(1)}, s32[16]{0:T(128)}, u32[]{:S(2)}) %copy-start.6) | copy-done | bytes 88
  7.9 20.7 %shard_map.95 = (f32[4,16,128]{2,1,0:T(8,128)S(1)}, f32[4,16,128]{2,1,0:T(8,128)S(1)}) custom-call(f32[4,16,128]{2,1,0:T(8,128)S(1)} %copy-done.1, f32[4,16,128]{2,1,0:T(8,128)S(1)} %copy-done.2, f32[4,16,128]{2,1,0:T(8,128)S(1)} %copy-done.3, f32[16,128]{1,0:T(8,128)S(1)} %copy-done.4, f32[16,128]{1,0:T(8,128)S(1)} %copy-done.5, ...), custom_call_target="tpu_custom_call" | custom-call | tf_op jit(solution)/shard_map/pallas_call | solution.py:435
  28.6 0.6 %copy.13 = f32[4,16,128]{2,1,0:T(8,128)} copy(f32[4,16,128]{2,1,0:T(8,128)S(1)} %get-tuple-element.4) | data formatting | bytes 65536
  29.2 0.6 %copy.14 = f32[4,16,128]{2,1,0:T(8,128)} copy(f32[4,16,128]{2,1,0:T(8,128)S(1)} %get-tuple-element.5) | data formatting | bytes 65536
Async XLA Ops:
  1.4 2.2 %copy-start = (f32[16,4,128,128]{3,2,1,0:T(8,128)S(1)}, f32[16,4,128,128]{3,2,1,0:T(8,128)}, u32[]{:S(2)}) copy-start(f32[16,4,128,128]{3,2,1,0:T(8,128)} %mat_hbm.1) | copy-start | bytes 12582916
  3.6 0.8 %copy-start.1 = (f32[4,16,128]{2,1,0:T(8,128)S(1)}, f32[4,16,128]{2,1,0:T(8,128)}, u32[]{:S(2)}) copy-start(f32[4,16,128]{2,1,0:T(8,128)} %x_hbm.1) | copy-start | bytes 98308
  4.3 0.8 %copy-start.2 = (f32[4,16,128]{2,1,0:T(8,128)S(1)}, f32[4,16,128]{2,1,0:T(8,128)}, u32[]{:S(2)}) copy-start(f32[4,16,128]{2,1,0:T(8,128)} %lam_hbm.1) | copy-start | bytes 98308
  5.1 0.8 %copy-start.3 = (f32[4,16,128]{2,1,0:T(8,128)S(1)}, f32[4,16,128]{2,1,0:T(8,128)}, u32[]{:S(2)}) copy-start(f32[4,16,128]{2,1,0:T(8,128)} %dem_hbm.1) | copy-start | bytes 98308
  5.9 0.7 %copy-start.4 = (f32[16,128]{1,0:T(8,128)S(1)}, f32[16,128]{1,0:T(8,128)}, u32[]{:S(2)}) copy-start(f32[16,128]{1,0:T(8,128)} %cost_hbm.1) | copy-start | bytes 24580
  6.5 0.7 %copy-start.5 = (f32[16,128]{1,0:T(8,128)S(1)}, f32[16,128]{1,0:T(8,128)}, u32[]{:S(2)}) copy-start(f32[16,128]{1,0:T(8,128)} %pen_hbm.1) | copy-start | bytes 24580
  7.2 0.7 %copy-start.6 = (s32[16]{0:T(128)S(1)}, s32[16]{0:T(128)}, u32[]{:S(2)}) copy-start(s32[16]{0:T(128)} %sec_hbm.1) | copy-start | bytes 196

commit v2 on v1

--- a/solution.py
+++ b/solution.py
@@ -199,7 +199,7 @@
         set_halo([zero] * HB, [zero] * HB)
 
     def forward_row(i):
-        lhs = jnp.concatenate([hl[cols[i, k]] for k in range(nnz)], axis=1).astype(jnp.bfloat16)
+        lhs = jnp.concatenate([hl[cols[k, i]] for k in range(nnz)], axis=1).astype(jnp.bfloat16)
         out = lax.dot_general(
             lhs, split[i], (((1,), (1,)), ((), ())), preferred_element_type=jnp.float32
         )
@@ -222,7 +222,7 @@
             term = both[:, k * blk : (k + 1) * blk]
             for o in range(-HB, HB + 1):
                 if o != 0:
-                    put(HB + i + o, jnp.where(cols[i, k] == HB + i + o, term, zero))
+                    put(HB + i + o, jnp.where(cols[k, i] == HB + i + o, term, zero))
 
     edge = list(range(HB)) + list(range(nb - HB, nb))
     inner = list(range(HB, nb - HB))
@@ -405,7 +405,7 @@
         V((nb, blk), f32),
         V((nb, blk), f32),
         V(mat.shape, f32),
-        pltpu.SMEM((nb, nnz), jnp.int32),
+        pltpu.SMEM((nnz, nb), jnp.int32),
         pltpu.SMEM((nb,), jnp.int32),
         V((nb, 2 * blk, nnz * blk), jnp.bfloat16),
         V((nb * R, blk), f32),
@@ -430,18 +430,18 @@
         dma((slots,)),
         dma((slots,)),
     ]
-    any_spec = pl.BlockSpec(memory_space=pl.ANY)
+    hbm_spec = pl.BlockSpec(memory_space=pltpu.HBM)
     vmem_spec = pl.BlockSpec(memory_space=pltpu.VMEM)
     return pl.pallas_call(
         functools.partial(kernel, nets, nodes),
         out_shape=(jax.ShapeDtypeStruct(x.shape, f32), jax.ShapeDtypeStruct(x.shape, f32)),
-        in_specs=[any_spec] * 8,
+        in_specs=[hbm_spec] * 8,
         out_specs=(vmem_spec, vmem_spec),
         scratch_shapes=scratch,
         compiler_params=pltpu.CompilerParams(
-            collective_id=0, has_side_effects=True, vmem_limit_bytes=40 << 20
+            collective_id=0, has_side_effects=True, vmem_limit_bytes=67_043_328
         ),
-    )(*args)
+    )(*args[:6], args[6].T, args[7])
 
 
 def solution(mesh):

time: 30.3 us -> 25.6 us (0.84)
  local copies, waits for them, and re-layouts: 8.5 us -> 2.75 us
  Pallas kernels: 20.7 us -> 22 us
    unnamed x17 -> x2, local copies, waits for them, and re-layouts: 8.5 us -> 2.75 us
    pallas_call x1, Pallas kernels: 20.7 us -> 22 us  [body(): pl.pallas_call(functools.partial(kernel, nets, nodes), out_shape=(jax.Sha...]
where the time goes in v2:
time: 25.6 us; the launch traced here: 25.4 us
  Pallas kernels  22 us (86%)
  local copies, waits for them, and re-layouts  2.75 us (11%)
  between operations  0.64 us (2%)
    pallas_call x1, Pallas kernels, body(): pl.pallas_call(functools.partial(kernel, nets, nodes), out_shape=(jax.Sha...  22 us
    unnamed x2, local copies, waits for them, and re-layouts  2.75 us

profile of v2, /device:TPU:0, one launch (start us, length us, event | category | flops | bytes accessed | tf_op | source)
XLA Modules:
  0.0 25.4 jit_solution(2292306762332331687)
XLA Ops:
  0.6 22.0 %shard_map.95 = (f32[4,16,128]{2,1,0:T(8,128)}, f32[4,16,128]{2,1,0:T(8,128)}) custom-call(f32[4,16,128]{2,1,0:T(8,128)} %x_hbm.1, f32[4,16,128]{2,1,0:T(8,128)} %lam_hbm.1, f32[4,16,128]{2,1,0:T(8,128)} %dem_hbm.1, f32[16,128]{1,0:T(8,128)} %cost_hbm.1, f32[16,128]{1,0:T(8,128)} %pen_hbm.1, f32[16,4,128,128]{3,2,1,0:T(8,128)} %mat_hbm.1, s32[4,16]{1,0:T(4,128)} %bitcast.1, ...), custom_call_target="tpu_custom_call" | custom-call | tf_op jit(solution)/shard_map/pallas_call | solution.py:435
  22.6 1.4 %copy.12 = f32[4,16,128]{2,1,0:T(8,128)} copy(f32[4,16,128]{2,1,0:T(8,128)} %get-tuple-element.4) | data formatting | bytes 65536
  24.0 1.4 %copy.13 = f32[4,16,128]{2,1,0:T(8,128)} copy(f32[4,16,128]{2,1,0:T(8,128)} %get-tuple-element.5) | data formatting | bytes 65536

commit v3 on v2

--- a/solution.py
+++ b/solution.py
@@ -33,8 +33,9 @@
     mat_hbm,
     col_hbm,
     sec_hbm,
-    cons_ref,
-    newm_ref,
+    sum_ref,
+    clip_ref,
+    size_ref,
     x_in,
     lam_in,
     dem_in,
@@ -377,11 +378,10 @@
         mine = mine + extra
         slot += len(masks)
     shared = group >= L
-    size = group.astype(jnp.float32)
     for s in range(L):
-        mean = jnp.where(shared, mine, sums[s]) / size
-        cons_ref[s] = mean
-        newm_ref[s] = lam_in[s] + pen_in[...] * (clipped[s] - mean)
+        sum_ref[s] = jnp.where(shared, mine, sums[s])
+        clip_ref[s] = clipped[s]
+    size_ref[...] = group.astype(jnp.float32)
 
 
 def body(*args):
@@ -432,16 +432,18 @@
     ]
     hbm_spec = pl.BlockSpec(memory_space=pltpu.HBM)
     vmem_spec = pl.BlockSpec(memory_space=pltpu.VMEM)
-    return pl.pallas_call(
+    sums, clipped, size = pl.pallas_call(
         functools.partial(kernel, nets, nodes),
-        out_shape=(jax.ShapeDtypeStruct(x.shape, f32), jax.ShapeDtypeStruct(x.shape, f32)),
+        out_shape=(V(x.shape, f32), V(x.shape, f32), V((nb, blk), f32)),
         in_specs=[hbm_spec] * 8,
-        out_specs=(vmem_spec, vmem_spec),
+        out_specs=(vmem_spec, vmem_spec, vmem_spec),
         scratch_shapes=scratch,
         compiler_params=pltpu.CompilerParams(
-            collective_id=0, has_side_effects=True, vmem_limit_bytes=67_043_328
+            collective_id=0, has_side_effects=True, vmem_limit_bytes=60_000_000
         ),
     )(*args[:6], args[6].T, args[7])
+    mean = sums / size[None]
+    return mean, args[1] + args[4][None] * (clipped - mean)
 
 
 def solution(mesh):

time: 25.6 us -> 22.8 us (0.89)
  local copies, waits for them, and re-layouts: 2.75 us -> 0.01 us
  other arithmetic: 0 us -> 0.64 us
  Pallas kernels: 22 us -> 21.4 us
    unnamed x2 -> x4, local copies, waits for them, and re-layouts: 2.75 us -> 0.01 us
    add x0 -> x1, other arithmetic: none -> 0.64 us  [body(): return (mean, args[1] + args[4][None] * (clipped - mean))]
    pallas_call x1, Pallas kernels: 22 us -> 21.4 us  [body(): pl.pallas_call(functools.partial(kernel, nets, nodes), out_shape=(V(x.sha...]
where the time goes in v3:
time: 22.8 us; the launch traced here: 22.7 us
  Pallas kernels  21.4 us (94%)
  between operations  0.67 us (3%)
  other arithmetic  0.64 us (3%)
    pallas_call x1, Pallas kernels, body(): pl.pallas_call(functools.partial(kernel, nets, nodes), out_shape=(V(x.sha...  21.4 us
    add x1, other arithmetic, body(): return (mean, args[1] + args[4][None] * (clipped - mean))  0.64 us

profile of v3, /device:TPU:0, one launch (start us, length us, event | category | flops | bytes accessed | tf_op | source)
XLA Modules:
  0.0 22.7 jit_solution(18003568263688771135)
XLA Ops:
  0.6 0.0 copy-start.1
  0.6 0.0 copy-start
  0.7 21.4 %shard_map.95 = (f32[4,16,128]{2,1,0:T(8,128)S(1)}, f32[4,16,128]{2,1,0:T(8,128)S(1)}, f32[16,128]{1,0:T(8,128)S(1)}) custom-call(f32[4,16,128]{2,1,0:T(8,128)} %x_hbm.1, f32[4,16,128]{2,1,0:T(8,128)} %lam_hbm.1, f32[4,16,128]{2,1,0:T(8,128)} %dem_hbm.1, f32[16,128]{1,0:T(8,128)} %cost_hbm.1, f32[16,128]{1,0:T(8,128)} %pen_hbm.1, ...), custom_call_target="tpu_custom_call" | custom-call | tf_op jit(solution)/shard_map/pallas_call | solution.py:435
  22.0 0.0 copy-done.1
  22.0 0.0 copy-done
  22.1 0.6 %multiply_add_fusion = (f32[4,16,128]{2,1,0:T(8,128)}, f32[4,16,128]{2,1,0:T(8,128)}) fusion(f32[4,16,128]{2,1,0:T(8,128)S(1)} %copy-done, f32[4,16,128]{2,1,0:T(8,128)S(1)} %get-tuple-element.7, f32[16,128]{1,0:T(8,128)S(1)} %copy-done.1, f32[4,16,128]{2,1,0:T(8,128)S(1)} %get-tuple-element.5, f32[16,128]{1,0:T(8,128)S(1)} %get-tuple-element.6), kind=kLoop, calls=%fused_computation | loop fusion | flops 32768 | bytes 180224 | tf_op jit(solution)/shard_map/add | solution.py:446
Async XLA Ops:
  0.6 21.4 %copy-start.1 = (f32[16,128]{1,0:T(8,128)S(1)}, f32[16,128]{1,0:T(8,128)}, u32[]{:S(2)}) copy-start(f32[16,128]{1,0:T(8,128)} %pen_hbm.1) | copy-start | bytes 24580
  0.6 21.4 %copy-start = (f32[4,16,128]{2,1,0:T(8,128)S(1)}, f32[4,16,128]{2,1,0:T(8,128)}, u32[]{:S(2)}) copy-start(f32[4,16,128]{2,1,0:T(8,128)} %lam_hbm.1) | copy-start | bytes 98308

commit v4 on v3

--- a/solution.py
+++ b/solution.py
@@ -131,13 +131,61 @@
                 a - hi.astype(jnp.float32)
             ).astype(jnp.bfloat16)
 
-    first_half = nb // 2
-
-    @pl.loop(0, first_half)
+    half = nb // 2
+    for copy in small:
+        copy.wait()
+
+    upper = lax.broadcasted_iota(jnp.int32, (R, blk), 0) < L
+
+    def halves(v):
+        hi = v.astype(jnp.bfloat16).astype(jnp.float32)
+        return jnp.where(upper, hi, v - hi)
+
+    for s in range(L):
+        for r in (s, s + L):
+            xv[pl.ds(r, nb, stride=R), :] = x_in[s]
+            bv[pl.ds(r, nb, stride=R), :] = dem_in[s]
+            dv[pl.ds(r, nb, stride=R), :] = cost_in[...] + lam_in[s]
+            penb[pl.ds(r, nb, stride=R), :] = pen_in[...]
+    for i in range(nb):
+        sec_rows[i : i + 1, :] = jnp.full((1, blk), secs[i], jnp.int32)
+        hl[HB + i] = halves(xv[i * R : (i + 1) * R, :])
+
+    def halo_of_rows(ref, rows):
+        return [
+            jnp.concatenate([ref[s, r : r + 1] for s in list(range(L)) * 2], axis=0) for r in rows
+        ]
+
+    zero = jnp.zeros((R, blk), jnp.float32)
+
+    def set_halo(low, high):
+        for j in range(HB):
+            hl[j] = halves(jnp.where(has_left, low[j], zero))
+            hl[HB + nb + j] = halves(jnp.where(has_right, high[j], zero))
+
+    def forward_row(i):
+        lhs = jnp.concatenate([hl[cols[k, i]] for k in range(nnz)], axis=1).astype(jnp.bfloat16)
+        out = lax.dot_general(
+            lhs, split[i], (((1,), (1,)), ((), ())), preferred_element_type=jnp.float32
+        )
+        both = out[:, :blk] + out[:, blk:]
+        return both + pltpu.roll(both, L, 0)
+
+    edge = list(range(HB)) + list(range(nb - HB, nb))
+    inner = list(range(HB, nb - HB))
+
+    w = [None] * nb
+
+    def first_product(rows_now):
+        for i in rows_now:
+            w[i] = bv[i * R : (i + 1) * R, :] - forward_row(i)
+
+    @pl.loop(0, half)
     def _(i):
         pltpu.make_async_copy(mat_hbm.at[i], mat_in.at[i], mat_sem.at[i]).wait()
         make_split(i)
 
+    first_product([i for i in inner if i < half])
     pl.semaphore_wait(barrier, count)
     x_sends = [
         pltpu.make_async_remote_copy(
@@ -152,45 +200,14 @@
     ]
     for copy in x_sends:
         copy.start()
-    for copy in small:
-        copy.wait()
-
-    upper = lax.broadcasted_iota(jnp.int32, (R, blk), 0) < L
-
-    def halves(v):
-        hi = v.astype(jnp.bfloat16).astype(jnp.float32)
-        return jnp.where(upper, hi, v - hi)
-
-    for s in range(L):
-        for r in (s, s + L):
-            xv[pl.ds(r, nb, stride=R), :] = x_in[s]
-            bv[pl.ds(r, nb, stride=R), :] = dem_in[s]
-            dv[pl.ds(r, nb, stride=R), :] = cost_in[...] + lam_in[s]
-            penb[pl.ds(r, nb, stride=R), :] = pen_in[...]
-    for i in range(nb):
-        sec_rows[i : i + 1, :] = jnp.full((1, blk), secs[i], jnp.int32)
-        hl[HB + i] = halves(xv[i * R : (i + 1) * R, :])
-
-    @pl.loop(first_half, nb)
+    @pl.loop(half, nb)
     def _(i):
         pltpu.make_async_copy(mat_hbm.at[i], mat_in.at[i], mat_sem.at[i]).wait()
         make_split(i)
 
+    first_product([i for i in inner if i >= half])
     for copy in x_sends:
         copy.wait()
-
-    def halo_of_rows(ref, rows):
-        return [
-            jnp.concatenate([ref[s, r : r + 1] for s in list(range(L)) * 2], axis=0) for r in rows
-        ]
-
-    zero = jnp.zeros((R, blk), jnp.float32)
-
-    def set_halo(low, high):
-        for j in range(HB):
-            hl[j] = halves(jnp.where(has_left, low[j], zero))
-            hl[HB + nb + j] = halves(jnp.where(has_right, high[j], zero))
-
     if nets > 1:
         set_halo(
             halo_of_rows(x_got.at[0], range(nb - HB, nb)),
@@ -199,13 +216,7 @@
     else:
         set_halo([zero] * HB, [zero] * HB)
 
-    def forward_row(i):
-        lhs = jnp.concatenate([hl[cols[k, i]] for k in range(nnz)], axis=1).astype(jnp.bfloat16)
-        out = lax.dot_general(
-            lhs, split[i], (((1,), (1,)), ((), ())), preferred_element_type=jnp.float32
-        )
-        both = out[:, :blk] + out[:, blk:]
-        return both + pltpu.roll(both, L, 0)
+    first_product(edge)
 
     def transpose_row(i, w, acc):
         h = halves(w)
@@ -224,9 +235,6 @@
             for o in range(-HB, HB + 1):
                 if o != 0:
                     put(HB + i + o, jnp.where(cols[k, i] == HB + i + o, term, zero))
-
-    edge = list(range(HB)) + list(range(nb - HB, nb))
-    inner = list(range(HB, nb - HB))
 
     def send(e, blocks, partial):
         for j, b in enumerate(blocks):
@@ -307,7 +315,6 @@
             ]
         return terms[0]
 
-    w = [bv[i * R : (i + 1) * R, :] - forward_row(i) for i in range(nb)]
     z = transposed(0, w, None)
     r0 = [z[i] - dv[i * R : (i + 1) * R, :] for i in range(nb)]
     part0 = add_all([v * v for v in r0])

time: 22.8 us -> 23.5 us (1.031)
  Pallas kernels: 21.4 us -> 22 us
    pallas_call x1, Pallas kernels: 21.4 us -> 22 us  [body(): pl.pallas_call(functools.partial(kernel, nets, nodes), out_shape=(V(x.sha...]
where the time goes in v4:
time: 23.5 us; the launch traced here: 23.3 us
  Pallas kernels  22 us (94%)
  between operations  0.67 us (3%)
  other arithmetic  0.64 us (3%)
    pallas_call x1, Pallas kernels, body(): pl.pallas_call(functools.partial(kernel, nets, nodes), out_shape=(V(x.sha...  22 us
    add x1, other arithmetic, body(): return (mean, args[1] + args[4][None] * (clipped - mean))  0.64 us

profile of v4, /device:TPU:0, one launch (start us, length us, event | category | flops | bytes accessed | tf_op | source)
XLA Modules:
  0.0 23.3 jit_solution(8489520964483542396)
XLA Ops:
  0.6 0.0 copy-start.1
  0.6 0.0 copy-start
  0.7 22.0 %shard_map.95 = (f32[4,16,128]{2,1,0:T(8,128)S(1)}, f32[4,16,128]{2,1,0:T(8,128)S(1)}, f32[16,128]{1,0:T(8,128)S(1)}) custom-call(f32[4,16,128]{2,1,0:T(8,128)} %x_hbm.1, f32[4,16,128]{2,1,0:T(8,128)} %lam_hbm.1, f32[4,16,128]{2,1,0:T(8,128)} %dem_hbm.1, f32[16,128]{1,0:T(8,128)} %cost_hbm.1, f32[16,128]{1,0:T(8,128)} %pen_hbm.1, ...), custom_call_target="tpu_custom_call" | custom-call | tf_op jit(solution)/shard_map/pallas_call | solution.py:442
  22.7 0.0 copy-done.1
  22.7 0.0 copy-done
  22.7 0.6 %multiply_add_fusion = (f32[4,16,128]{2,1,0:T(8,128)}, f32[4,16,128]{2,1,0:T(8,128)}) fusion(f32[4,16,128]{2,1,0:T(8,128)S(1)} %copy-done, f32[4,16,128]{2,1,0:T(8,128)S(1)} %get-tuple-element.7, f32[16,128]{1,0:T(8,128)S(1)} %copy-done.1, f32[4,16,128]{2,1,0:T(8,128)S(1)} %get-tuple-element.5, f32[16,128]{1,0:T(8,128)S(1)} %get-tuple-element.6), kind=kLoop, calls=%fused_computation | loop fusion | flops 32768 | bytes 180224 | tf_op jit(solution)/shard_map/add | solution.py:453
Async XLA Ops:
  0.6 22.0 %copy-start.1 = (f32[16,128]{1,0:T(8,128)S(1)}, f32[16,128]{1,0:T(8,128)}, u32[]{:S(2)}) copy-start(f32[16,128]{1,0:T(8,128)} %pen_hbm.1) | copy-start | bytes 24580
  0.6 22.0 %copy-start = (f32[4,16,128]{2,1,0:T(8,128)S(1)}, f32[4,16,128]{2,1,0:T(8,128)}, u32[]{:S(2)}) copy-start(f32[4,16,128]{2,1,0:T(8,128)} %lam_hbm.1) | copy-start | bytes 98308

commit v5 on v3

--- a/solution.py
+++ b/solution.py
@@ -131,13 +131,6 @@
                 a - hi.astype(jnp.float32)
             ).astype(jnp.bfloat16)
 
-    first_half = nb // 2
-
-    @pl.loop(0, first_half)
-    def _(i):
-        pltpu.make_async_copy(mat_hbm.at[i], mat_in.at[i], mat_sem.at[i]).wait()
-        make_split(i)
-
     pl.semaphore_wait(barrier, count)
     x_sends = [
         pltpu.make_async_remote_copy(
@@ -171,7 +164,7 @@
         sec_rows[i : i + 1, :] = jnp.full((1, blk), secs[i], jnp.int32)
         hl[HB + i] = halves(xv[i * R : (i + 1) * R, :])
 
-    @pl.loop(first_half, nb)
+    @pl.loop(0, nb)
     def _(i):
         pltpu.make_async_copy(mat_hbm.at[i], mat_in.at[i], mat_sem.at[i]).wait()
         make_split(i)

time: 22.8 us -> 22.9 us (level)
  no operation moved by 1% of the time
where the time goes in v5:
time: 22.9 us; the launch traced here: 22.8 us
  Pallas kernels  21.5 us (94%)
  between operations  0.67 us (3%)
  other arithmetic  0.64 us (3%)
    pallas_call x1, Pallas kernels, body(): pl.pallas_call(functools.partial(kernel, nets, nodes), out_shape=(V(x.sha...  21.5 us
    add x1, other arithmetic, body(): return (mean, args[1] + args[4][None] * (clipped - mean))  0.64 us

profile of v5, /device:TPU:0, one launch (start us, length us, event | category | flops | bytes accessed | tf_op | source)
XLA Modules:
  0.0 22.8 jit_solution(3875023300401298096)
XLA Ops:
  0.6 0.0 copy-start.1
  0.6 0.0 copy-start
  0.7 21.5 %shard_map.95 = (f32[4,16,128]{2,1,0:T(8,128)S(1)}, f32[4,16,128]{2,1,0:T(8,128)S(1)}, f32[16,128]{1,0:T(8,128)S(1)}) custom-call(f32[4,16,128]{2,1,0:T(8,128)} %x_hbm.1, f32[4,16,128]{2,1,0:T(8,128)} %lam_hbm.1, f32[4,16,128]{2,1,0:T(8,128)} %dem_hbm.1, f32[16,128]{1,0:T(8,128)} %cost_hbm.1, f32[16,128]{1,0:T(8,128)} %pen_hbm.1, ...), custom_call_target="tpu_custom_call" | custom-call | tf_op jit(solution)/shard_map/pallas_call | solution.py:428
  22.1 0.0 copy-done.1
  22.2 0.0 copy-done
  22.2 0.6 %multiply_add_fusion = (f32[4,16,128]{2,1,0:T(8,128)}, f32[4,16,128]{2,1,0:T(8,128)}) fusion(f32[4,16,128]{2,1,0:T(8,128)S(1)} %copy-done, f32[4,16,128]{2,1,0:T(8,128)S(1)} %get-tuple-element.7, f32[16,128]{1,0:T(8,128)S(1)} %copy-done.1, f32[4,16,128]{2,1,0:T(8,128)S(1)} %get-tuple-element.5, f32[16,128]{1,0:T(8,128)S(1)} %get-tuple-element.6), kind=kLoop, calls=%fused_computation | loop fusion | flops 32768 | bytes 180224 | tf_op jit(solution)/shard_map/add | solution.py:439
Async XLA Ops:
  0.6 21.5 %copy-start.1 = (f32[16,128]{1,0:T(8,128)S(1)}, f32[16,128]{1,0:T(8,128)}, u32[]{:S(2)}) copy-start(f32[16,128]{1,0:T(8,128)} %pen_hbm.1) | copy-start | bytes 24580
  0.6 21.5 %copy-start = (f32[4,16,128]{2,1,0:T(8,128)S(1)}, f32[4,16,128]{2,1,0:T(8,128)}, u32[]{:S(2)}) copy-start(f32[4,16,128]{2,1,0:T(8,128)} %lam_hbm.1) | copy-start | bytes 98308
